TPU v7x, 512 devices: a whole 4x4x16 slice. The times are simulated.
512 devices in a mesh: wide: 64 (over z, x), narrow: 8 (over y, core).
Axes of the slice: x: 4, y: 4, z: 16, core: 2. Of those that a mesh axis runs over, the one named last changes fastest.
Arguments:
- sublevel_symbol_entries: bfloat16 [1024, 4, 4096], P('wide', None, 'narrow'), may hold values from -160 to 160
- prior_symbol_memory: bfloat16 [1024, 4096], P('wide', 'narrow'), may hold values from -6 to 6
- entry_scaling_multiplier: float32 [4096], P('narrow'), may hold values from 0.25 to 1.75
- entry_scaling_offset: float32 [4096], P('narrow'), may hold values from -4 to 4
- learned_blending: float32 [6, 4096], P(None, 'narrow'), may hold values from 0 to 1
- blending_lowering_coefficients: bfloat16 [4096, 160], P('narrow'), may hold values from -0.09375 to 0.09375
- blending_raising_coefficients: bfloat16 [5, 32, 4096], P(None, None, 'narrow'), may hold values from -1 to 1
- fading_lowering_coefficients: bfloat16 [4096, 64], P('narrow'), may hold values from -0.09375 to 0.09375
- fading_raising_coefficients: bfloat16 [64, 4096], P(None, 'wide'), may hold values from -0.75 to 0.75
- learned_fading: float32 [4096], P('wide'), may hold values from -6 to 1
- immediate_item_premium: float32 [4096], P('wide'), may hold values from -3 to 3
- acceptor_projection: bfloat16 [4096, 4096], P('narrow', 'wide'), may hold values from -0.09375 to 0.09375
- lookup_projection: bfloat16 [4096, 4096], P('narrow', 'wide'), may hold values from -0.09375 to 0.09375
- payload_projection: bfloat16 [4096, 4096], P('narrow', 'wide'), may hold values from -0.09375 to 0.09375
- gating_projection: bfloat16 [4096, 4096], P('narrow', 'wide'), may hold values from -0.09375 to 0.09375
- emission_projection: bfloat16 [4096, 4096], P(None, 'wide'), may hold values from -0.09375 to 0.09375
- group_scaling_multiplier: float32 [4096], P('wide'), may hold values from 0.25 to 1.75
- group_scaling_offset: float32 [4096], P('wide'), may hold values from -4 to 4
- dialogue_group_memory: float32 [262144, 1024], P('wide', 'narrow'), may hold values from -6 to 6
Outputs:
- mixing_output: bfloat16 [1024, 4, 4096], P('narrow', None, 'wide')
- final_state: float32 [262144, 1024], P('wide', 'narrow')
All inputs are finite; a program needn't handle non-finite values.
Results may differ from a plain program's by a relative error of at most 0.034.
Values may be sent and summed in bfloat16 or wider, within the bound.
A program may use at most 64 MiB of HBM per device.

v0:
```python
import jax
import jax.numpy as jnp
from jax import lax
from jax.sharding import PartitionSpec as P

CHANNEL_SPAN = 64
FEATURE_EXTENT = 4096


def per_device(
    sublevel_symbol_entries,
    prior_symbol_memory,
    entry_scaling_multiplier,
    entry_scaling_offset,
    learned_blending,
    blending_lowering_coefficients,
    blending_raising_coefficients,
    fading_lowering_coefficients,
    fading_raising_coefficients,
    learned_fading,
    immediate_item_premium,
    acceptor_projection,
    lookup_projection,
    payload_projection,
    gating_projection,
    emission_projection,
    group_scaling_multiplier,
    group_scaling_offset,
    dialogue_group_memory,
):
    rank = blending_raising_coefficients.shape[1]
    narrow_rows = dialogue_group_memory.shape[1]
    local_width = emission_projection.shape[1]
    group_partition = local_width // CHANNEL_SPAN
    weights = (acceptor_projection, lookup_projection, payload_projection, gating_projection)
    shift_gathered = lax.all_gather(prior_symbol_memory, "wide", axis=0, tiled=True)

    def channel_set_first(block):
        return block.reshape(narrow_rows, group_partition, CHANNEL_SPAN).transpose(1, 2, 0)

    present_symbol = dialogue_group_memory.reshape(
        group_partition, CHANNEL_SPAN, CHANNEL_SPAN, narrow_rows
    )
    previous_rows = prior_symbol_memory
    previous_all = shift_gathered
    results = []
    for index in range(sublevel_symbol_entries.shape[1]):
        floats = sublevel_symbol_entries[:, index : index + 1].astype(jnp.float32)
        totals, squares = lax.psum((jnp.sum(floats, -1), jnp.sum(floats * floats, -1)), "narrow")
        prepare_center = totals[..., None] / FEATURE_EXTENT
        spread = squares[..., None] / FEATURE_EXTENT - prepare_center * prepare_center
        normed = (
            (floats - prepare_center) * lax.rsqrt(spread + 1e-05) * entry_scaling_multiplier
            + entry_scaling_offset
        ).astype(jnp.bfloat16)
        previous = jnp.concatenate([previous_rows[:, None], normed[:, :-1]], 1)
        prepare_normalized_float = normed.astype(jnp.float32)
        prepare_shifted_input = previous.astype(jnp.float32) - prepare_normalized_float
        blended = (prepare_normalized_float + prepare_shifted_input * learned_blending[0]).astype(
            jnp.bfloat16
        )
        partial_mix = jnp.einsum(
            "smd,dr->smr",
            blended,
            blending_lowering_coefficients,
            preferred_element_type=jnp.float32,
        )
        hidden_activation = jnp.tanh(lax.psum(partial_mix, "narrow")).astype(jnp.bfloat16)
        decay_shift = jnp.einsum(
            "smr,rd->smd",
            hidden_activation[..., :rank],
            blending_raising_coefficients[0],
            preferred_element_type=jnp.float32,
        )
        decay_mix = (
            prepare_normalized_float + prepare_shifted_input * (learned_blending[1] + decay_shift)
        ).astype(jnp.bfloat16)
        partial_decay = jnp.einsum(
            "smd,dr->smr",
            decay_mix,
            fading_lowering_coefficients,
            preferred_element_type=jnp.float32,
        )
        decay_hidden = jnp.tanh(lax.psum(partial_decay, "narrow")).astype(jnp.bfloat16)
        small = jnp.concatenate([hidden_activation[..., rank:], decay_hidden], -1)
        prepare_normed_all = lax.all_gather(normed, "wide", axis=0, tiled=True)
        prepare_small_all = lax.all_gather(small, "wide", axis=0, tiled=True)
        normed, normed_all, small_all = (normed, prepare_normed_all, prepare_small_all)
        project_previous_all = previous_all[:, None]
        normalized_float = normed_all.astype(jnp.float32)
        shifted_input = project_previous_all.astype(jnp.float32) - normalized_float
        term_results = []
        for selector_index in range(4):
            low_rank_update = jnp.einsum(
                "smr,rd->smd",
                small_all[..., selector_index * rank : (selector_index + 1) * rank],
                blending_raising_coefficients[selector_index + 1],
                preferred_element_type=jnp.float32,
            )
            mixed_input = (
                normalized_float
                + shifted_input * (learned_blending[selector_index + 2] + low_rank_update)
            ).astype(jnp.bfloat16)
            term_results.append(
                jnp.einsum(
                    "smd,de->sme",
                    mixed_input,
                    weights[selector_index],
                    preferred_element_type=jnp.float32,
                )
            )
        project_transformed_outcome = lax.psum_scatter(
            jnp.concatenate(term_results, -1).astype(jnp.bfloat16),
            "narrow",
            scatter_dimension=0,
            tiled=True,
        ).astype(jnp.float32)
        rows_start = lax.axis_index("narrow") * narrow_rows
        decay_rows = lax.dynamic_slice_in_dim(
            small_all[..., 4 * rank :], rows_start, narrow_rows, 0
        )
        decay_log = learned_fading + jnp.einsum(
            "smr,rd->smd",
            decay_rows,
            fading_raising_coefficients,
            preferred_element_type=jnp.float32,
        )
        shrink_coefficient = jnp.exp(-jnp.exp(decay_log))
        recurrence_present_symbol = present_symbol
        each_group_reward = immediate_item_premium.reshape(group_partition, CHANNEL_SPAN)
        present_acceptor = channel_set_first(project_transformed_outcome[:, 0, :local_width])
        key_now = channel_set_first(
            project_transformed_outcome[:, 0, local_width : 2 * local_width]
        )
        value_now = channel_set_first(
            project_transformed_outcome[:, 0, 2 * local_width : 3 * local_width]
        )
        gate_now = project_transformed_outcome[:, 0, 3 * local_width :]
        forget_now = channel_set_first(shrink_coefficient[:, 0])
        dyadic_tensor = key_now[:, :, None, :] * value_now[:, None, :, :]
        memory_retrieval = jnp.sum(
            present_acceptor[:, :, None, :]
            * (recurrence_present_symbol + each_group_reward[:, :, None, None] * dyadic_tensor),
            1,
        )
        recurrence_present_symbol = (
            forget_now[:, :, None, :] * recurrence_present_symbol + dyadic_tensor
        )
        center = jnp.mean(memory_retrieval, 1, keepdims=True)
        offset = memory_retrieval - center
        scaled = offset * lax.rsqrt(jnp.mean(offset * offset, 1, keepdims=True) + 0.00064)
        squashed_vector = scaled.transpose(2, 0, 1).reshape(narrow_rows, local_width)
        pieces = [
            (
                (squashed_vector * group_scaling_multiplier + group_scaling_offset)
                * jax.nn.silu(gate_now)
            ).astype(jnp.bfloat16)
        ]
        present_symbol = recurrence_present_symbol
        gated = jnp.stack(pieces, 1)
        results.append(
            jnp.einsum(
                "smc,ce->sme",
                lax.all_gather(gated, "wide", axis=2, tiled=True),
                emission_projection,
                preferred_element_type=jnp.float32,
            ).astype(jnp.bfloat16)
        )
        previous_rows = normed[:, 0]
        previous_all = normed_all[:, 0]
    mixing_output = jnp.concatenate(results, 1)
    return (
        mixing_output,
        present_symbol.reshape(group_partition * CHANNEL_SPAN * CHANNEL_SPAN, narrow_rows),
    )


def solution(mesh):
    placed = (
        P("wide", None, "narrow"),
        P("wide", "narrow"),
        P("narrow"),
        P("narrow"),
        P(None, "narrow"),
        P("narrow", None),
        P(None, None, "narrow"),
        P("narrow", None),
        P(None, "wide"),
        P("wide"),
        P("wide"),
        P("narrow", "wide"),
        P("narrow", "wide"),
        P("narrow", "wide"),
        P("narrow", "wide"),
        P(None, "wide"),
        P("wide"),
        P("wide"),
        P("wide", "narrow"),
    )
    return jax.shard_map(
        per_device,
        mesh=mesh,
        in_specs=placed,
        out_specs=(P("narrow", None, "wide"), P("wide", "narrow")),
        check_vma=False,
    )
```

profile of v0, /device:TPU:8, one launch (start us, length us, event | category | flops | bytes accessed | tf_op | source)
XLA Modules:
  0.0 1447.9 jit_solution(15403730953367358589)
XLA Ops:
  7.3 1.1 fusion.287
  8.7 14.8 %all-reduce.2 = (f32[16,1]{0,1:T(1,128)S(1)}, f32[16,1]{0,1:T(1,128)S(1)}, f32[16,1]{0,1:T(1,128)S(1)}, f32[16,1]{0,1:T(1,128)S(1)}, f32[16,1]{0,1:T(1,128)S(1)}...) all-reduce(f32[16,1]{0,1:T(1,128)S(1)} %bitcast.846, ...), channel_id=1, replica_groups=mesh['wide'=64,'narrow'=8] {'narrow'}, use_global_device_ids=true, to_apply=%region_13.14 | all-reduce | flops 128 | bytes 1024 | tf_op jit(solution)/shard_map/psum | solution.py:49
  23.6 1.4 fusion.145
  28.6 1.1 convolution_bitcast_fusion
  29.7 1.1 convolution_bitcast_fusion.1
  30.9 1.1 convolution_bitcast_fusion.2
  32.0 1.1 convolution_bitcast_fusion.3
  33.1 24.0 %all-reduce.1 = (f32[16,1,160]{2,0,1:T(8,128)S(1)}, f32[16,1,160]{2,0,1:T(8,128)S(1)}, f32[16,1,160]{2,0,1:T(8,128)S(1)}, f32[16,1,160]{2,0,1:T(8,128)S(1)}) all-reduce(f32[16,1,160]{2,0,1:T(8,128)S(1)} %convolution_bitcast_fusion.1, ...), channel_id=1, replica_groups=mesh['wide'=64,'narrow'=8] {'narrow'}, use_global_device_ids=true, to_apply=%region_24.25 | all-reduce | flops 10240 | bytes 81920 | tf_op jit(solution)/shard_map/psum | solution.py:68
  57.2 1.1 convolution_bitcast_fusion.5
  58.3 1.1 convolution_bitcast_fusion.6
  61.9 24.4 %all-reduce = (f32[16,1,64]{2,0,1:T(8,128)S(1)}, f32[16,1,64]{2,0,1:T(8,128)S(1)}, f32[16,1,64]{2,0,1:T(8,128)S(1)}, f32[16,1,64]{2,0,1:T(8,128)S(1)}) all-reduce(f32[16,1,64]{2,0,1:T(8,128)S(1)} %convolution_bitcast_fusion.5, f32[16,1,64]{2,0,1:T(8,128)S(1)} %convolution_bitcast_fusion.6, ...), channel_id=1, replica_groups=mesh['wide'=64,'narrow'=8] {'narrow'}, use_global_device_ids=true, to_apply=%region_25.26 | all-reduce | flops 4096 | bytes 32768 | tf_op jit(solution)/shard_map/psum | solution.py:84
  86.4 103.3 %all_gather.50 = bf16[1024,1,192]{2,0,1:T(8,128)(2,1)S(1)} all-gather(bf16[16,1,192]{2,0,1:T(8,128)(2,1)S(1)} %pad_maximum_fusion.4), channel_id=1, replica_groups=mesh['wide'=64,'narrow'=8] {'wide'}, dimensions={0}, use_global_device_ids=true | all-gather | bytes 399360 | tf_op jit(solution)/shard_map/all_gather | solution.py:87
  189.7 99.2 %all_gather.41 = bf16[1024,1,192]{2,0,1:T(8,128)(2,1)S(1)} all-gather(bf16[16,1,192]{2,0,1:T(8,128)(2,1)S(1)} %pad_maximum_fusion.1), channel_id=1, replica_groups=mesh['wide'=64,'narrow'=8] {'wide'}, dimensions={0}, use_global_device_ids=true | all-gather | bytes 399360 | tf_op jit(solution)/shard_map/all_gather | solution.py:87
  288.9 97.0 %all_gather.44 = bf16[1024,1,192]{2,0,1:T(8,128)(2,1)S(1)} all-gather(bf16[16,1,192]{2,0,1:T(8,128)(2,1)S(1)} %pad_maximum_fusion.2), channel_id=1, replica_groups=mesh['wide'=64,'narrow'=8] {'wide'}, dimensions={0}, use_global_device_ids=true | all-gather | bytes 399360 | tf_op jit(solution)/shard_map/all_gather | solution.py:87
  385.9 99.0 %all_gather.47 = bf16[1024,1,192]{2,0,1:T(8,128)(2,1)S(1)} all-gather(bf16[16,1,192]{2,0,1:T(8,128)(2,1)S(1)} %pad_maximum_fusion.3), channel_id=1, replica_groups=mesh['wide'=64,'narrow'=8] {'wide'}, dimensions={0}, use_global_device_ids=true | all-gather | bytes 399360 | tf_op jit(solution)/shard_map/all_gather | solution.py:87
  487.3 2.4 fusion.75
  489.7 2.4 fusion.74
  492.2 2.3 fusion.73
  494.5 2.3 fusion.72
  498.1 81.7 %all-gather.10.cloned.1.call-done = bf16[1024,1,512]{2,0,1:T(8,128)(2,1)} async-done(((bf16[16,1,512]{2,0,1:T(8,128)(2,1)}), bf16[1024,1,512]{2,0,1:T(8,128)(2,1)}) %all-gather.10.cloned.1.call-update) | async-done | bytes 1048592 | tf_op jit(solution)/shard_map/all_gather | solution.py:86
  579.9 2.4 fusion.63
  582.3 2.4 fusion.62
  584.7 2.4 fusion.61
  587.1 2.3 fusion.60
  590.5 127.2 %all-gather.16.cloned.1.call-done = bf16[1024,1,512]{2,0,1:T(8,128)(2,1)} async-done(((bf16[16,1,512]{2,0,1:T(8,128)(2,1)}), bf16[1024,1,512]{2,0,1:T(8,128)(2,1)}) %all-gather.16.cloned.1.call-update) | async-done | bytes 1048592 | tf_op jit(solution)/shard_map/all_gather | solution.py:86
  717.7 2.4 fusion.67
  720.2 2.1 fusion.66
  722.2 2.0 fusion.65
  724.3 2.0 fusion.64
  727.6 2.1 fusion.71
  729.7 2.1 fusion.70
  731.8 2.1 fusion.69
  733.9 2.0 fusion.68
  737.2 14.9 %reduce-scatter.19.cloned.1.call-done = bf16[128,256]{1,0:T(8,128)(2,1)} async-done(((bf16[1024,256]{1,0:T(8,128)(2,1)}), bf16[128,256]{1,0:T(8,128)(2,1)}) %reduce-scatter.19.cloned.1.call-update) | async-done | bytes 65552
  753.0 39.6 %reduce-scatter.13.cloned.1.call-done = bf16[128,256]{1,0:T(8,128)(2,1)} async-done(((bf16[1024,256]{1,0:T(8,128)(2,1)}), bf16[128,256]{1,0:T(8,128)(2,1)}) %reduce-scatter.13.cloned.1.call-update) | async-done | bytes 65552
  793.6 39.4 %reduce-scatter.15.cloned.1.call-done = bf16[128,256]{1,0:T(8,128)(2,1)} async-done(((bf16[1024,256]{1,0:T(8,128)(2,1)}), bf16[128,256]{1,0:T(8,128)(2,1)}) %reduce-scatter.15.cloned.1.call-update) | async-done | bytes 65552
  834.0 40.1 %reduce-scatter.17.cloned.1.call-done = bf16[128,256]{1,0:T(8,128)(2,1)} async-done(((bf16[1024,256]{1,0:T(8,128)(2,1)}), bf16[128,256]{1,0:T(8,128)(2,1)}) %reduce-scatter.17.cloned.1.call-update) | async-done | bytes 65552
  877.3 2.1 fusion.8
  879.4 1.9 fusion.28
  881.3 2.1 fusion.43
  886.4 138.9 %all-gather.14.cloned.1.call-done = bf16[128,1,4096]{0,2,1:T(8,128)(2,1)} async-done(((bf16[128,1,64]{0,2,1:T(8,128)(2,1)}), bf16[128,1,4096]{0,2,1:T(8,128)(2,1)}) %all-gather.14.cloned.1.call-update) | async-done | bytes 1048592 | tf_op jit(solution)/shard_map/all_gather | solution.py:164
  1025.4 1.5 fusion.108
  1026.9 136.4 %all-gather.18.cloned.1.call-done = bf16[128,1,4096]{0,2,1:T(8,128)(2,1)} async-done(((bf16[128,1,64]{0,2,1:T(8,128)(2,1)}), bf16[128,1,4096]{0,2,1:T(8,128)(2,1)}) %all-gather.18.cloned.1.call-update) | async-done | bytes 1048592 | tf_op jit(solution)/shard_map/all_gather | solution.py:164
  1163.4 1.5 fusion.109
  1164.9 136.3 %all-gather.22.cloned.1.call-done = bf16[128,1,4096]{0,2,1:T(8,128)(2,1)} async-done(((bf16[128,1,64]{0,2,1:T(8,128)(2,1)}), bf16[128,1,4096]{0,2,1:T(8,128)(2,1)}) %all-gather.22.cloned.1.call-update) | async-done | bytes 1048592 | tf_op jit(solution)/shard_map/all_gather | solution.py:164
  1301.2 1.5 fusion.110
  1302.7 136.4 %all-gather.26.cloned.1.call-done = bf16[128,1,4096]{0,2,1:T(8,128)(2,1)} async-done(((bf16[128,1,64]{0,2,1:T(8,128)(2,1)}), bf16[128,1,4096]{0,2,1:T(8,128)(2,1)}) %all-gather.26.cloned.1.call-update) | async-done | bytes 1048592 | tf_op jit(solution)/shard_map/all_gather | solution.py:164
  1439.2 1.5 fusion.111
  (146 shorter events, 23.5 us)
Async XLA Ops:
  7.2 1018.2 %copy-start = (bf16[4096,64]{0,1:T(8,128)(2,1)S(1)}, bf16[4096,64]{0,1:T(8,128)(2,1)}, u32[]{:S(2)}) copy-start(bf16[4096,64]{0,1:T(8,128)(2,1)} %param.34) | copy-start | bytes 1572868
  7.2 52.3 %copy-start.4 = (bf16[16,512]{1,0:T(8,128)(2,1)S(1)}, bf16[16,512]{1,0:T(8,128)(2,1)}, u32[]{:S(2)}) copy-start(bf16[16,512]{1,0:T(8,128)(2,1)} %param.20) | copy-start | bytes 49156
  7.2 52.3 %copy-start.2 = (bf16[512,64]{0,1:T(8,128)(2,1)S(1)}, bf16[512,64]{0,1:T(8,128)(2,1)}, u32[]{:S(2)}) copy-start(bf16[512,64]{0,1:T(8,128)(2,1)} %param.26) | copy-start | bytes 196612
  7.2 54.5 %copy-start.7 = (f32[64]{0:T(128)S(1)}, f32[64]{0:T(128)}, u32[]{:S(2)}) copy-start(f32[64]{0:T(128)} %param.29) | copy-start | bytes 772
  7.2 480.1 %all-gather.24.cloned.1.call-start = ((), (), s32[]{:S(2)}) async-start(), calls=%async_computation.11 | async-start | bytes 1064960 | tf_op jit(solution)/shard_map/all_gather | solution.py:86
  25.0 462.3 %all-gather.20.cloned.1.call-start = ((), (), s32[]{:S(2)}) async-start(), calls=%async_computation.9 | async-start | bytes 1064960 | tf_op jit(solution)/shard_map/all_gather | solution.py:86
  25.7 472.4 %all-gather.12.cloned.1.call-start = ((), (), s32[]{:S(2)}) async-start(), calls=%async_computation.5 | async-start | bytes 1064960 | tf_op jit(solution)/shard_map/all_gather | solution.py:36
  26.5 553.4 %all-gather.10.cloned.1.call-start = ((), (), s32[]{:S(2)}) async-start(), calls=%async_computation.4 | async-start | bytes 1064960 | tf_op jit(solution)/shard_map/all_gather | solution.py:86
  27.1 690.7 %all-gather.16.cloned.1.call-start = ((), (), s32[]{:S(2)}) async-start(), calls=%async_computation.7 | async-start | bytes 1064960 | tf_op jit(solution)/shard_map/all_gather | solution.py:86
  27.6 724.4 %reduce-scatter.19.cloned.1.call-start = ((), (), s32[]{:S(2)}) async-start(), calls=%async_computation.16 | async-start | bytes 589824
  86.3 399.3 %copy-start.3 = (bf16[64,64]{1,0:T(8,128)(2,1)S(1)}, bf16[64,64]{1,0:T(8,128)(2,1)}, u32[]{:S(2)}) copy-start(bf16[64,64]{1,0:T(8,128)(2,1)} %param.27) | copy-start | bytes 24580
  86.4 399.3 %copy-start.6 = (f32[64]{0:T(128)S(1)}, f32[64]{0:T(128)}, u32[]{:S(2)}) copy-start(f32[64]{0:T(128)} %param.28) | copy-start | bytes 772
  489.7 2.5 copy-start.5
  489.7 2.5 copy-start.15
  497.8 84.4 %copy-start.13 = (bf16[512,64]{0,1:T(8,128)(2,1)S(1)}, bf16[512,64]{0,1:T(8,128)(2,1)}, u32[]{:S(2)}) copy-start(bf16[512,64]{0,1:T(8,128)(2,1)} %param.32) | copy-start | bytes 196612
  497.9 294.8 %reduce-scatter.13.cloned.1.call-start = ((), (), s32[]{:S(2)}) async-start(), calls=%async_computation.13 | async-start | bytes 589824
  582.2 2.4 copy-start.16
  584.7 2.4 copy-start.18
  589.4 128.4 %copy-start.12 = (bf16[512,64]{0,1:T(8,128)(2,1)S(1)}, bf16[512,64]{0,1:T(8,128)(2,1)}, u32[]{:S(2)}) copy-start(bf16[512,64]{0,1:T(8,128)(2,1)} %param.33) | copy-start | bytes 196612
  590.4 242.6 %reduce-scatter.15.cloned.1.call-start = ((), (), s32[]{:S(2)}) async-start(), calls=%async_computation.14 | async-start | bytes 589824
  717.7 2.5 copy-start.11
  726.2 1.3 copy-start.10
  727.3 2.3 copy-start.14
  727.3 146.8 %reduce-scatter.17.cloned.1.call-start = ((), (), s32[]{:S(2)}) async-start(), calls=%async_computation.15 | async-start | bytes 589824
  729.6 2.1 copy-start.17
  731.7 2.1 copy-start.19
  736.9 288.5 %all-gather.14.cloned.1.call-start = ((), (), s32[]{:S(2)}) async-start(), calls=%async_computation.6 | async-start | bytes 1064960 | tf_op jit(solution)/shard_map/all_gather | solution.py:164
  875.7 1.6 copy-start.1
  881.3 2.3 copy-start.8
  881.3 2.3 copy-start.9
  884.4 279.0 %all-gather.18.cloned.1.call-start = ((), (), s32[]{:S(2)}) async-start(), calls=%async_computation.8 | async-start | bytes 1064960 | tf_op jit(solution)/shard_map/all_gather | solution.py:164
  885.1 416.1 %all-gather.22.cloned.1.call-start = ((), (), s32[]{:S(2)}) async-start(), calls=%async_computation.10 | async-start | bytes 1064960 | tf_op jit(solution)/shard_map/all_gather | solution.py:164
  885.7 553.5 %all-gather.26.cloned.1.call-start = ((), (), s32[]{:S(2)}) async-start(), calls=%async_computation.12 | async-start | bytes 1064960 | tf_op jit(solution)/shard_map/all_gather | solution.py:164
Sparse Core Ops, SparseCore 0:
  25.1 140.8 all-gather.23
  168.9 134.9 all-gather.19
  306.8 135.0 all-gather.11
  444.7 135.1 all-gather.9
  582.7 134.9 all-gather.15
  720.4 31.6 reduce-scatter.18
  755.1 37.5 reduce-scatter.12
  795.5 37.4 reduce-scatter.14
  836.6 37.5 reduce-scatter.16
  884.5 140.8 all-gather.13
  1028.3 134.9 all-gather.17
  1166.2 134.9 all-gather.21
  1304.1 134.9 all-gather.25
where the time goes:
time: 1450 us
  waiting for transfers between devices  896 us (62%)
  blocking collectives  462 us (32%)
  matrix products  51.9 us (4%)
  between operations  14.7 us (1%)
    all_gather x4, waiting for transfers between devices, per_device(): lax.all_gather(gated, 'wide', axis=2, tiled=True)  548 us
    all_gather x4, blocking collectives, per_device(): prepare_small_all = lax.all_gather(small, 'wide', axis=0, tiled=True)  398 us
    all_gather x4, waiting for transfers between devices, per_device(): prepare_normed_all = lax.all_gather(normed, 'wide', axis=0, tiled=True)  209 us
    unnamed x17, waiting for transfers between devices  138 us
    dot_general x16, matrix products, per_device(): jnp.einsum('smd,de->sme', mixed_input, weights[selector_index], preferred...  35.5 us
  transfers between devices with their start and end apart: 13, of which 10 were waited for; matrix products, arithmetic and copies ran while one was open for 4% of the time, Pallas kernels for 0%

commit v1 on v0

--- a/solution.py
+++ b/solution.py
@@ -5,6 +5,12 @@
 
 CHANNEL_SPAN = 64
 FEATURE_EXTENT = 4096
+
+
+def gather_by_exchange(x, axis, dim):
+    size = lax.axis_size(axis)
+    repeats = [size if d == dim else 1 for d in range(x.ndim)]
+    return lax.all_to_all(jnp.tile(x, repeats), axis, split_axis=dim, concat_axis=dim, tiled=True)
 
 
 def per_device(
@@ -161,7 +167,7 @@
         results.append(
             jnp.einsum(
                 "smc,ce->sme",
-                lax.all_gather(gated, "wide", axis=2, tiled=True),
+                gather_by_exchange(gated, "wide", 2),
                 emission_projection,
                 preferred_element_type=jnp.float32,
             ).astype(jnp.bfloat16)

time: 1450 us -> 1210 us (0.83)
  the two profiles are of different devices: /device:TPU:8 before, /device:TPU:24 now
where the time goes in v1:
time: 1210 us; the launch traced here: 1200 us
  blocking collectives  461 us (38%)
  waiting for transfers between devices  403 us (33%)
  local copies, waits for them, and re-layouts  131 us (11%)
  other arithmetic  104 us (9%)
  matrix products  52.7 us (4%)
  starting transfers between devices  35.3 us (3%)
  between operations  15 us (1%)
    all_gather x4, blocking collectives, per_device(): prepare_small_all = lax.all_gather(small, 'wide', axis=0, tiled=True)  398 us
    unnamed x13, waiting for transfers between devices  146 us
    all_gather x4, waiting for transfers between devices, per_device(): prepare_normed_all = lax.all_gather(normed, 'wide', axis=0, tiled=True)  128 us
    unnamed x8, other arithmetic  93.7 us
    all_gather x1, waiting for transfers between devices, per_device(): lax.all_gather(prior_symbol_memory, 'wide', axis=0, tiled=True)  71.7 us
    another operation x8, local copies, waits for them, and re-layouts, gather_by_exchange(): jnp.tile(x, repeats)  67.9 us
    all_to_all x4, waiting for transfers between devices, gather_by_exchange(): lax.all_to_all(jnp.tile(x, repeats), axis, split_axis=dim, concat_axis=di...  56.7 us
    unnamed x67, local copies, waits for them, and re-layouts  44.1 us
  transfers between devices with their start and end apart: 13, of which 10 were waited for; matrix products, arithmetic and copies ran while one was open for 18% of the time, Pallas kernels for 0%

profile of v1, /device:TPU:24, one launch (start us, length us, event | category | flops | bytes accessed | tf_op | source)
XLA Modules:
  0.0 1200.9 jit_solution(9012834429346026926)
XLA Ops:
  8.7 14.1 %all-reduce.2 = (f32[16,1]{0,1:T(1,128)S(1)}, f32[16,1]{0,1:T(1,128)S(1)}, f32[16,1]{0,1:T(1,128)S(1)}, f32[16,1]{0,1:T(1,128)S(1)}, f32[16,1]{0,1:T(1,128)S(1)}...) all-reduce(f32[16,1]{0,1:T(1,128)S(1)} %bitcast.898, ...), channel_id=1, replica_groups=mesh['wide'=64,'narrow'=8] {'narrow'}, use_global_device_ids=true, to_apply=%region_13.14 | all-reduce | flops 128 | bytes 1024 | tf_op jit(solution)/shard_map/psum | solution.py:55
  32.4 24.9 %all-reduce.1 = (f32[16,1,160]{2,0,1:T(8,128)S(1)}, f32[16,1,160]{2,0,1:T(8,128)S(1)}, f32[16,1,160]{2,0,1:T(8,128)S(1)}, f32[16,1,160]{2,0,1:T(8,128)S(1)}) all-reduce(f32[16,1,160]{2,0,1:T(8,128)S(1)} %convolution_bitcast_fusion.1, ...), channel_id=1, replica_groups=mesh['wide'=64,'narrow'=8] {'narrow'}, use_global_device_ids=true, to_apply=%region_24.25 | all-reduce | flops 10240 | bytes 81920 | tf_op jit(solution)/shard_map/psum | solution.py:74
  61.9 23.3 %all-reduce = (f32[16,1,64]{2,0,1:T(8,128)S(1)}, f32[16,1,64]{2,0,1:T(8,128)S(1)}, f32[16,1,64]{2,0,1:T(8,128)S(1)}, f32[16,1,64]{2,0,1:T(8,128)S(1)}) all-reduce(f32[16,1,64]{2,0,1:T(8,128)S(1)} %convolution_bitcast_fusion.5, f32[16,1,64]{2,0,1:T(8,128)S(1)} %convolution_bitcast_fusion.6, ...), channel_id=1, replica_groups=mesh['wide'=64,'narrow'=8] {'narrow'}, use_global_device_ids=true, to_apply=%region_25.26 | all-reduce | flops 4096 | bytes 32768 | tf_op jit(solution)/shard_map/psum | solution.py:90
  85.2 103.1 %all_gather.33 = bf16[1024,1,192]{2,0,1:T(8,128)(2,1)S(1)} all-gather(bf16[16,1,192]{2,0,1:T(8,128)(2,1)S(1)} %pad_maximum_fusion.3), channel_id=1, replica_groups=mesh['wide'=64,'narrow'=8] {'wide'}, dimensions={0}, use_global_device_ids=true | all-gather | bytes 399360 | tf_op jit(solution)/shard_map/all_gather | solution.py:93
  188.4 99.3 %all_gather.31 = bf16[1024,1,192]{2,0,1:T(8,128)(2,1)S(1)} all-gather(bf16[16,1,192]{2,0,1:T(8,128)(2,1)S(1)} %pad_maximum_fusion.2), channel_id=1, replica_groups=mesh['wide'=64,'narrow'=8] {'wide'}, dimensions={0}, use_global_device_ids=true | all-gather | bytes 399360 | tf_op jit(solution)/shard_map/all_gather | solution.py:93
  287.7 96.8 %all_gather.29 = bf16[1024,1,192]{2,0,1:T(8,128)(2,1)S(1)} all-gather(bf16[16,1,192]{2,0,1:T(8,128)(2,1)S(1)} %pad_maximum_fusion.1), channel_id=1, replica_groups=mesh['wide'=64,'narrow'=8] {'wide'}, dimensions={0}, use_global_device_ids=true | all-gather | bytes 399360 | tf_op jit(solution)/shard_map/all_gather | solution.py:93
  384.6 99.3 %all_gather.35 = bf16[1024,1,192]{2,0,1:T(8,128)(2,1)S(1)} all-gather(bf16[16,1,192]{2,0,1:T(8,128)(2,1)S(1)} %pad_maximum_fusion.4), channel_id=1, replica_groups=mesh['wide'=64,'narrow'=8] {'wide'}, dimensions={0}, use_global_device_ids=true | all-gather | bytes 399360 | tf_op jit(solution)/shard_map/all_gather | solution.py:93
  486.4 2.4 fusion.71
  488.8 2.4 fusion.70
  491.2 2.4 fusion.69
  493.7 2.3 fusion.68
  497.3 2.4 fusion.67
  499.8 2.4 fusion.66
  502.2 2.4 fusion.65
  508.0 71.7 %all-gather.8.cloned.1.call-done = bf16[1024,512]{1,0:T(8,128)(2,1)} async-done(((bf16[16,512]{1,0:T(8,128)(2,1)}), bf16[1024,512]{1,0:T(8,128)(2,1)}) %all-gather.8.cloned.1.call-update) | async-done | bytes 1048592 | tf_op jit(solution)/shard_map/all_gather | solution.py:42
  579.7 2.4 fusion.63
  582.1 2.4 fusion.62
  584.5 2.4 fusion.61
  590.3 127.8 %all-gather.14.cloned.1.call-done = bf16[1024,1,512]{2,0,1:T(8,128)(2,1)} async-done(((bf16[16,1,512]{2,0,1:T(8,128)(2,1)}), bf16[1024,1,512]{2,0,1:T(8,128)(2,1)}) %all-gather.14.cloned.1.call-update) | async-done | bytes 1048592 | tf_op jit(solution)/shard_map/all_gather | solution.py:92
  718.1 2.3 fusion.75
  727.7 25.3 %reduce-scatter.17.cloned.1.call-done = bf16[128,256]{1,0:T(8,128)(2,1)} async-done(((bf16[1024,256]{1,0:T(8,128)(2,1)}), bf16[128,256]{1,0:T(8,128)(2,1)}) %reduce-scatter.17.cloned.1.call-update) | async-done | bytes 65552
  754.0 39.6 %reduce-scatter.15.cloned.1.call-done = bf16[128,256]{1,0:T(8,128)(2,1)} async-done(((bf16[1024,256]{1,0:T(8,128)(2,1)}), bf16[128,256]{1,0:T(8,128)(2,1)}) %reduce-scatter.15.cloned.1.call-update) | async-done | bytes 65552
  794.6 39.4 %reduce-scatter.13.cloned.1.call-done = bf16[128,256]{1,0:T(8,128)(2,1)} async-done(((bf16[1024,256]{1,0:T(8,128)(2,1)}), bf16[128,256]{1,0:T(8,128)(2,1)}) %reduce-scatter.13.cloned.1.call-update) | async-done | bytes 65552
  835.0 39.6 %reduce-scatter.19.cloned.1.call-done = bf16[128,256]{1,0:T(8,128)(2,1)} async-done(((bf16[1024,256]{1,0:T(8,128)(2,1)}), bf16[128,256]{1,0:T(8,128)(2,1)}) %reduce-scatter.19.cloned.1.call-update) | async-done | bytes 65552
  884.6 16.7 %copy.89 = bf16[128,1,4096]{0,1,2:T(2,128)(2,1)S(1)} copy(bf16[128,1,4096]{0,2,1:T(8,128)(2,1)S(1)} %bitcast.885) | data formatting | bytes 2097152 | tf_op jit(solution)/shard_map/tile | solution.py:13
  901.8 23.4 %reduce.28 = bf16[4096,128]{1,0:T(8,128)(2,1)} reduce(bf16[4096,1,128]{2,1,0:T(2,128)(2,1)S(1)} %bitcast.881, bf16[]{:T(256)} %broadcast.911), dimensions={1}, to_apply=%bitcast.872.reduce_sub_computation | reduce | bytes 2097154
  927.4 16.3 %all-to-all-start.3 = ((bf16[64,2,4096]{2,1,0:T(2,128)(2,1)}), bf16[64,2,4096]{2,1,0:T(2,128)(2,1)}, u32[]{:S(2)}, u32[]{:S(2)}) async-start(bf16[64,2,4096]{2,1,0:T(2,128)(2,1)} %reshape.1586), calls=%async_computation.3 | async-start | bytes 2097152 | tf_op jit(solution)/shard_map/all_to_all | solution.py:13
  943.9 16.7 %copy.90 = bf16[128,1,4096]{0,1,2:T(2,128)(2,1)S(1)} copy(bf16[128,1,4096]{0,2,1:T(8,128)(2,1)S(1)} %bitcast.886) | data formatting | bytes 2097152 | tf_op jit(solution)/shard_map/tile | solution.py:13
  960.7 23.4 %reduce.29 = bf16[4096,128]{1,0:T(8,128)(2,1)} reduce(bf16[4096,1,128]{2,1,0:T(2,128)(2,1)S(1)} %bitcast.883, bf16[]{:T(256)} %broadcast.911), dimensions={1}, to_apply=%bitcast.873.reduce_sub_computation | reduce | bytes 2097154
  986.2 13.9 %all-to-all-done.3 = bf16[64,2,4096]{2,1,0:T(2,128)(2,1)} async-done(((bf16[64,2,4096]{2,1,0:T(2,128)(2,1)}), bf16[64,2,4096]{2,1,0:T(2,128)(2,1)}, u32[]{:S(2)}, u32[]{:S(2)}) %all-to-all-start.3) | async-done | bytes 1048608 | tf_op jit(solution)/shard_map/all_to_all | solution.py:13
  1000.1 6.1 all-to-all-start.2
  1006.4 16.7 %copy.91 = bf16[128,1,4096]{0,1,2:T(2,128)(2,1)S(1)} copy(bf16[128,1,4096]{0,2,1:T(8,128)(2,1)S(1)} %bitcast.887) | data formatting | bytes 2097152 | tf_op jit(solution)/shard_map/tile | solution.py:13
  1023.2 23.4 %reduce.30 = bf16[4096,128]{1,0:T(8,128)(2,1)} reduce(bf16[4096,1,128]{2,1,0:T(2,128)(2,1)S(1)} %bitcast.884, bf16[]{:T(256)} %broadcast.911), dimensions={1}, to_apply=%bitcast.874.reduce_sub_computation | reduce | bytes 2097154
  1048.7 12.3 %all-to-all-done.2 = bf16[64,2,4096]{2,1,0:T(2,128)(2,1)} async-done(((bf16[64,2,4096]{2,1,0:T(2,128)(2,1)}), bf16[64,2,4096]{2,1,0:T(2,128)(2,1)}, u32[]{:S(2)}, u32[]{:S(2)}) %all-to-all-start.2) | async-done | bytes 1048608 | tf_op jit(solution)/shard_map/all_to_all | solution.py:13
  1061.0 6.3 all-to-all-start.1
  1067.5 16.7 %copy.92 = bf16[128,1,4096]{0,1,2:T(2,128)(2,1)S(1)} copy(bf16[128,1,4096]{0,2,1:T(8,128)(2,1)S(1)} %bitcast.888) | data formatting | bytes 2097152 | tf_op jit(solution)/shard_map/tile | solution.py:13
  1084.3 23.4 %reduce.31 = bf16[4096,128]{1,0:T(8,128)(2,1)} reduce(bf16[4096,1,128]{2,1,0:T(2,128)(2,1)S(1)} %bitcast.882, bf16[]{:T(256)} %broadcast.911), dimensions={1}, to_apply=%bitcast.875.reduce_sub_computation | reduce | bytes 2097154
  1109.9 11.9 all-to-all-done.1
  1121.8 6.1 all-to-all-start
  1127.9 6.5 reshape.1587
  1134.4 3.8 copy.52
  1138.2 6.5 reshape.1589
  1144.7 3.9 copy.49
  1148.6 6.5 reshape.1591
  1155.0 3.8 copy.46
  1162.8 18.6 %all-to-all-done = bf16[64,2,4096]{2,1,0:T(2,128)(2,1)} async-done(((bf16[64,2,4096]{2,1,0:T(2,128)(2,1)}), bf16[64,2,4096]{2,1,0:T(2,128)(2,1)}, u32[]{:S(2)}, u32[]{:S(2)}) %all-to-all-start) | async-done | bytes 1048608 | tf_op jit(solution)/shard_map/all_to_all | solution.py:13
  1181.5 6.5 reshape.1593
  1187.9 3.8 copy.43
  (177 shorter events, 62.5 us)
Async XLA Ops:
  7.2 1151.7 %copy-start = (bf16[4096,64]{0,1:T(8,128)(2,1)S(1)}, bf16[4096,64]{0,1:T(8,128)(2,1)}, u32[]{:S(2)}) copy-start(bf16[4096,64]{0,1:T(8,128)(2,1)} %param.34) | copy-start | bytes 1572868
  7.2 52.5 %copy-start.5 = (bf16[16,512]{1,0:T(8,128)(2,1)S(1)}, bf16[16,512]{1,0:T(8,128)(2,1)}, u32[]{:S(2)}) copy-start(bf16[16,512]{1,0:T(8,128)(2,1)} %param.20) | copy-start | bytes 49156
  7.2 52.5 %copy-start.3 = (bf16[512,64]{0,1:T(8,128)(2,1)S(1)}, bf16[512,64]{0,1:T(8,128)(2,1)}, u32[]{:S(2)}) copy-start(bf16[512,64]{0,1:T(8,128)(2,1)} %param.26) | copy-start | bytes 196612
  7.2 479.2 %all-gather.10.cloned.1.call-start = ((), (), s32[]{:S(2)}) async-start(), calls=%async_computation.10 | async-start | bytes 1064960 | tf_op jit(solution)/shard_map/all_gather | solution.py:92
  24.3 462.1 %all-gather.12.cloned.1.call-start = ((), (), s32[]{:S(2)}) async-start(), calls=%async_computation.11 | async-start | bytes 1064960 | tf_op jit(solution)/shard_map/all_gather | solution.py:92
  25.0 472.3 %all-gather.6.cloned.1.call-start = ((), (), s32[]{:S(2)}) async-start(), calls=%async_computation.8 | async-start | bytes 1064960 | tf_op jit(solution)/shard_map/all_gather | solution.py:92
  25.8 553.9 %all-gather.8.cloned.1.call-start = ((), (), s32[]{:S(2)}) async-start(), calls=%async_computation.9 | async-start | bytes 1064960 | tf_op jit(solution)/shard_map/all_gather | solution.py:42
  26.3 691.8 %all-gather.14.cloned.1.call-start = ((), (), s32[]{:S(2)}) async-start(), calls=%async_computation.12 | async-start | bytes 1064960 | tf_op jit(solution)/shard_map/all_gather | solution.py:92
  26.9 726.1 %reduce-scatter.17.cloned.1.call-start = ((), (), s32[]{:S(2)}) async-start(), calls=%async_computation.15 | async-start | bytes 589824
  59.7 424.1 %copy-start.10 = (f32[64]{0:T(128)S(1)}, f32[64]{0:T(128)}, u32[]{:S(2)}) copy-start(f32[64]{0:T(128)} %param.29) | copy-start | bytes 772
  85.2 399.5 %copy-start.4 = (bf16[64,64]{1,0:T(8,128)(2,1)S(1)}, bf16[64,64]{1,0:T(8,128)(2,1)}, u32[]{:S(2)}) copy-start(bf16[64,64]{1,0:T(8,128)(2,1)} %param.27) | copy-start | bytes 24580
  85.2 399.5 %copy-start.9 = (f32[64]{0:T(128)S(1)}, f32[64]{0:T(128)}, u32[]{:S(2)}) copy-start(f32[64]{0:T(128)} %param.28) | copy-start | bytes 772
  488.8 2.4 copy-start.17
  491.2 2.5 copy-start.21
  496.0 1.3 copy-start.14
  497.1 2.7 copy-start.6
  497.1 2.7 copy-start.15
  497.1 296.5 %reduce-scatter.15.cloned.1.call-start = ((), (), s32[]{:S(2)}) async-start(), calls=%async_computation.14 | async-start | bytes 589824
  499.7 2.4 copy-start.18
  502.1 2.4 copy-start.22
  506.8 72.8 %copy-start.7 = (bf16[5,32,512]{2,1,0:T(8,128)(2,1)S(1)}, bf16[5,32,512]{2,1,0:T(8,128)(2,1)}, u32[]{:S(2)}) copy-start(bf16[5,32,512]{2,1,0:T(8,128)(2,1)} %param.25) | copy-start | bytes 491524
  507.9 74.2 %copy-start.16 = (bf16[512,64]{0,1:T(8,128)(2,1)S(1)}, bf16[512,64]{0,1:T(8,128)(2,1)}, u32[]{:S(2)}) copy-start(bf16[512,64]{0,1:T(8,128)(2,1)} %param.32) | copy-start | bytes 196612
  507.9 326.0 %reduce-scatter.13.cloned.1.call-start = ((), (), s32[]{:S(2)}) async-start(), calls=%async_computation.13 | async-start | bytes 589824
  582.1 2.4 copy-start.19
  584.5 2.4 copy-start.8
  584.5 2.4 copy-start.23
  590.2 130.2 %copy-start.13 = (bf16[1024,1,512]{2,0,1:T(8,128)(2,1)S(1)}, bf16[1024,1,512]{2,0,1:T(8,128)(2,1)}, u32[]{:S(2)}) copy-start(bf16[1024,1,512]{2,0,1:T(8,128)(2,1)} %all-gather.12.cloned.1.call-done) | copy-start | bytes 3145732
  590.3 284.3 %reduce-scatter.19.cloned.1.call-start = ((), (), s32[]{:S(2)}) async-start(), calls=%async_computation.16 | async-start | bytes 589824
  720.4 2.1 copy-start.20
  722.5 2.1 copy-start.24
  876.1 1.6 copy-start.1
  881.9 2.3 copy-start.11
  881.9 2.3 copy-start.12
  927.4 72.7 %all-to-all-start.3 = ((bf16[64,2,4096]{2,1,0:T(2,128)(2,1)}), bf16[64,2,4096]{2,1,0:T(2,128)(2,1)}, u32[]{:S(2)}, u32[]{:S(2)}) async-start(bf16[64,2,4096]{2,1,0:T(2,128)(2,1)} %reshape.1586), calls=%async_computation.3 | async-start | bytes 2097152 | tf_op jit(solution)/shard_map/all_to_all | solution.py:13
  1000.1 60.9 %all-to-all-start.2 = ((bf16[64,2,4096]{2,1,0:T(2,128)(2,1)}), bf16[64,2,4096]{2,1,0:T(2,128)(2,1)}, u32[]{:S(2)}, u32[]{:S(2)}) async-start(bf16[64,2,4096]{2,1,0:T(2,128)(2,1)} %reshape.1588), calls=%async_computation.2 | async-start | bytes 2097152 | tf_op jit(solution)/shard_map/all_to_all | solution.py:13
  1061.0 60.7 %all-to-all-start.1 = ((bf16[64,2,4096]{2,1,0:T(2,128)(2,1)}), bf16[64,2,4096]{2,1,0:T(2,128)(2,1)}, u32[]{:S(2)}, u32[]{:S(2)}) async-start(bf16[64,2,4096]{2,1,0:T(2,128)(2,1)} %reshape.1590), calls=%async_computation.1 | async-start | bytes 2097152 | tf_op jit(solution)/shard_map/all_to_all | solution.py:13
  1121.8 59.7 %all-to-all-start = ((bf16[64,2,4096]{2,1,0:T(2,128)(2,1)}), bf16[64,2,4096]{2,1,0:T(2,128)(2,1)}, u32[]{:S(2)}, u32[]{:S(2)}) async-start(bf16[64,2,4096]{2,1,0:T(2,128)(2,1)} %reshape.1592), calls=%async_computation | async-start | bytes 2097152 | tf_op jit(solution)/shard_map/all_to_all | solution.py:13
  1158.8 3.5 copy-start.2
Sparse Core Ops, SparseCore 0:
  24.4 141.3 all-gather.9
  168.7 134.9 all-gather.11
  306.7 134.9 all-gather.5
  444.5 135.0 all-gather.7
  583.0 135.0 all-gather.13
  721.3 31.6 reduce-scatter.16
  756.0 37.5 reduce-scatter.14
  796.4 37.5 reduce-scatter.12
  837.0 37.5 reduce-scatter.18
